TPU v7x, 32 devices: a whole 2x2x4 slice. The times are simulated.
32 devices in a mesh: blk: 2 (over y), sector: 16 (over z, x, core).
Axes of the slice: x: 2, y: 2, z: 4, core: 2. Of those that a mesh axis runs over, the one named last changes fastest.
Arguments:
- state: float32 [5, 6, 6, 6, 4096], P(None, None, None, None, ('blk', 'sector')), may hold values from -6 to 6
- mean_flow: float32 [2, 4], replicated, may hold values from 0.2 to 1
- sector_offset: int32 [2], replicated, may hold values from 0 to 15
- frac_index: int32 [2], replicated, may hold values from 0 to 31
Outputs:
- new_state: float32 [5, 6, 6, 6, 4096], P(None, None, None, None, ('blk', 'sector'))
All inputs are finite; a program needn't handle non-finite values.
Results may differ from a plain program's by a relative error of at most 0.0003.
Values sent between devices are 32-bit elements; how exact they have to be, the bound alone decides.
A program may use at most 192 MiB of HBM per device.

v0:
```python
import functools
import math

import jax
import jax.numpy as jnp
import numpy as np
from jax import lax
from jax.experimental import pallas as pl
from jax.experimental.pallas import tpu as pltpu
from jax.sharding import PartitionSpec as P

FRACS = 4
EA = 8
ER = 4
EZ = 4
TIME_STEP = 0.02
V = 5
N = 6
LANES = 128
SLAB = EA * ER
TRACE_ROWS = 48
f32 = jnp.float32
MESH = pl.DeviceIdType.MESH


def lobatto_points():
    outer = math.sqrt(1.0 / 3.0 + 2.0 * math.sqrt(7.0) / 21.0)
    inner = math.sqrt(1.0 / 3.0 - 2.0 * math.sqrt(7.0) / 21.0)
    return np.array([-1.0, -outer, -inner, inner, outer, 1.0])


def derivative_matrix(points):
    number = points.shape[0]
    bary = np.array(
        [
            1.0 / np.prod([points[c] - points[o] for o in range(number) if o != c])
            for c in range(number)
        ]
    )
    matrix = np.zeros((number, number))
    for t in range(number):
        for s in range(number):
            if t != s:
                matrix[t, s] = bary[s] / bary[t] / (points[t] - points[s])
    return matrix


POINTS = lobatto_points()
DMAT = derivative_matrix(POINTS)
LIFT = N * (N - 1) / 2.0
HALF = 0.5 * LIFT


def stages_of(count):
    digits = []
    left = count
    while left > 1:
        radix = 4 if left % 4 == 0 else 2
        left //= radix
        digits.append((left, radix))
    return digits


def roll(x, by):
    by = by % LANES
    return x if by == 0 else pltpu.roll(x, by, 1)


def tile(v, a, b):
    return pl.multiple_of(((v * N + a) * N + b) * 8, 8)


def get(ref, v, a, b):
    return ref[pl.ds(tile(v, a, b), 8), :]


def choose(digit, options):
    out = options[0]
    for k in range(1, len(options)):
        out = jnp.where(digit == k, options[k], out)
    return out


def face(v, a, c):
    return pl.ds((v * N + a) * N * 8 + c, N, stride=8)


def by_sublane(values, rows):
    index = lax.broadcasted_iota(jnp.int32, (rows, LANES), 0)
    out = jnp.zeros((rows, LANES), f32)
    for k, value in enumerate(values):
        out = jnp.where(index == k, f32(value), out)
    return out


def kernel(
    sectors,
    flow_ref,
    offset_ref,
    frac_ref,
    dtab_ref,
    state_ref,
    out_ref,
    u_ref,
    w_ref,
    west_out,
    east_out,
    west_in,
    east_in,
    trace_out,
    hop_in,
    pair_in,
    send_sem,
    recv_sem,
):
    stages = stages_of(sectors)
    row = lax.axis_index("blk")
    me = lax.axis_index("sector")
    is_rotor = row == 0
    last_radix = stages[-1][1]

    def at(flip, off):
        return (1 - row if flip else row, lax.rem(me + off + sectors, sectors))

    targets = [(0, -1)]
    for s, (stride, radix) in enumerate(stages):
        flip = 1 if s == 0 else 0
        span = range(radix) if s == 0 else range(1, radix)
        if s == len(stages) - 1:
            span = range(1, radix + 1)
        for h in span:
            if (flip, h * stride) not in targets:
                targets.append((flip, h * stride))
    barrier = pltpu.get_barrier_semaphore()
    for flip, off in targets:
        pl.semaphore_signal(barrier, inc=1, device_id=at(flip, -off), device_id_type=MESH)

    lane = lax.broadcasted_iota(jnp.int32, (8, LANES), 1)
    lane6 = lane[:N]
    slot6 = lane6 % EA
    radial = (lane // EA) % ER
    s1 = 2.0 / (1.0 + (radial.astype(f32) + 0.5) / ER)
    s1_6 = s1[:N]

    def pick(k):
        return jnp.where(is_rotor, flow_ref[0, k], flow_ref[1, k])

    speed = [pick(k) for k in range(3)]
    sound = pick(3)
    other_axial = jnp.where(is_rotor, flow_ref[1, 2], flow_ref[0, 2])
    other_sound = jnp.where(is_rotor, flow_ref[1, 3], flow_ref[0, 3])
    top_sound = jnp.maximum(flow_ref[0, 3], flow_ref[1, 3])
    spread = [
        jnp.maximum(jnp.abs(flow_ref[0, k]), jnp.abs(flow_ref[1, k])) + top_sound for k in range(3)
    ]
    dcols = [by_sublane(DMAT[:, j], 8) for j in range(N)]
    own_a = jnp.where(is_rotor, N - 1, 0)

    def load_state(a, carry):
        for v in range(V):
            for b in range(N):
                u_ref[pl.ds(tile(v, a, b), N), :] = state_ref[v, a, b]
        return carry

    lax.fori_loop(0, N, load_state, 0)

    def pack(ref):
        for v in range(V):
            left = jnp.zeros((N, LANES), f32)
            right = jnp.zeros((N, LANES), f32)
            for a in range(N):
                left = jnp.where(slot6 == a, roll(ref[face(v, a, 0), :], a), left)
                right = jnp.where(slot6 == a, roll(ref[face(v, a, N - 1), :], a - EA + 1), right)
            west_out[v, pl.ds(0, N), :] = left
            east_out[v, pl.ds(0, N), :] = right
        quarter = lane6 // SLAB
        turned = jnp.where(is_rotor, (quarter + 1) % 4, quarter)
        for t in range(8):
            merged = jnp.zeros((N, LANES), f32)
            for q in range(4):
                n = 4 * t + q
                if n < V * N:
                    here = ref[pl.ds(tile(n // N, own_a, n % N), N), :]
                    merged = jnp.where(turned == q, roll(here, SLAB * q), merged)
            trace_out[pl.ds(N * t, N), :] = jnp.where(is_rotor, roll(merged, SLAB), merged)

    def copy(section, k, src, dst, target):
        return pltpu.make_async_remote_copy(
            src_ref=src,
            dst_ref=dst,
            send_sem=send_sem.at[section, k],
            recv_sem=recv_sem.at[section, k],
            device_id=target,
            device_id_type=MESH,
        )

    def send_first(section):
        copies = [
            copy(section, 2 + h, trace_out, hop_in.at[section, 0, h], at(1, h * stages[0][0]))
            for h in range(stages[0][1])
        ]
        halos = [
            copy(section, 0, west_out, west_in.at[section], at(0, -1)),
            copy(section, 1, east_out, east_in.at[section], at(0, 1)),
        ]
        for c in copies + halos:
            c.start()
        return copies, halos

    def forward(section, copies):
        amount = jnp.where(
            is_rotor,
            lax.rem(2 * sectors - offset_ref[section] - 1, sectors),
            lax.rem(offset_ref[section], sectors),
        )
        sem = 2 + stages[0][1]
        for s in range(1, len(stages)):
            for c in copies:
                c.wait()
            stride_before, radix_before = stages[s - 1]
            digit = lax.rem(amount // stride_before, radix_before)
            chosen = choose(digit, [hop_in[section, s - 1, h] for h in range(radix_before)])
            stride, radix = stages[s]
            if s == len(stages) - 1:
                dst, span = pair_in.at[section], range(1, radix + 1)
            else:
                dst, span = hop_in.at[section, s], range(1, radix)
            dst[0] = chosen
            copies = []
            for h in span:
                copies.append(copy(section, sem, dst.at[0], dst.at[h], at(0, h * stride)))
                sem += 1
            for c in copies:
                c.start()
        return copies, lax.rem(amount, last_radix)

    def volume(src, dst, base, scale):
        k1 = -scale * s1 * speed[0]
        c1 = -scale * s1 * sound
        k2 = jnp.full((8, LANES), -2.0 * scale * speed[1], f32)
        k3 = jnp.full((8, LANES), -2.0 * scale * speed[2], f32)
        c2 = jnp.full((8, LANES), -2.0 * scale * sound, f32)

        def at_b(b, carry):
            row_b = [dtab_ref[b, j] for j in range(N)]
            for a in range(N):
                kept = {}
                zero_sum = None
                for v in range(V):
                    start = tile(v, a, b)
                    g1 = dcols[0] * src[pl.ds(start, 1), :]
                    for j in range(1, N):
                        g1 = g1 + dcols[j] * src[pl.ds(start + j, 1), :]
                    g2 = row_b[0] * get(src, v, a, 0)
                    for j in range(1, N):
                        g2 = g2 + row_b[j] * get(src, v, a, j)
                    g3 = None
                    for j in range(N):
                        if j != a:
                            term = f32(DMAT[a, j]) * get(src, v, j, b)
                            g3 = term if g3 is None else g3 + term
                    total = base(v, a, b) + k1 * g1 + k2 * g2 + k3 * g3
                    if v == 0:
                        kept = {1: g1, 2: g2, 3: g3}
                        zero_sum = total
                        continue
                    if v == 1:
                        total = total + c1 * kept[1]
                        zero_sum = zero_sum + c1 * g1
                    if v == 2:
                        total = total + c2 * kept[2]
                        zero_sum = zero_sum + c2 * g2
                    if v == 3:
                        total = total + c2 * kept[3]
                        zero_sum = zero_sum + c2 * g3
                    dst[pl.ds(start, 8), :] = total
                dst[pl.ds(tile(0, a, b), 8), :] = zero_sum
            return carry

        lax.fori_loop(0, N, at_b, 0)

    def jumps(outside, inside, direction, sign, factor, along, acoustic):
        result = []
        for v in range(V):
            flux = along * outside[v]
            if v == 0:
                flux = flux + acoustic * outside[direction]
            if v == direction:
                flux = flux + acoustic * outside[0]
            gap = outside[v] if inside is None else outside[v] - inside[v]
            result.append(factor * (sign * flux + spread[direction - 1] * gap))
        return result

    def inner_faces(src, dst, scale):
        def azimuthal(a, carry):
            lows = [src[face(v, a, 0), :] for v in range(V)]
            highs = [src[face(v, a, N - 1), :] for v in range(V)]
            before = [jnp.where(slot6 == 0, 0.0, roll(x, 1)) for x in highs]
            after = [jnp.where(slot6 == EA - 1, 0.0, roll(x, -1)) for x in lows]
            factor = scale * HALF * s1_6
            for c, out, ins, sign in ((0, before, lows, 1.0), (N - 1, after, highs, -1.0)):
                for v, x in enumerate(jumps(out, ins, 1, sign, factor, speed[0], sound)):
                    dst[face(v, a, c), :] = dst[face(v, a, c), :] + x
            return carry

        lax.fori_loop(0, N, azimuthal, 0)

        def radial_faces(a, carry):
            lows = [get(src, v, a, 0) for v in range(V)]
            highs = [get(src, v, a, N - 1) for v in range(V)]
            below = [
                jnp.where(radial == 0, -lows[v] if v == 2 else lows[v], roll(highs[v], EA))
                for v in range(V)
            ]
            above = [
                jnp.where(radial == ER - 1, -highs[v] if v == 2 else highs[v], roll(lows[v], -EA))
                for v in range(V)
            ]
            factor = scale * LIFT
            for b, out, ins, sign in ((0, below, lows, 1.0), (N - 1, above, highs, -1.0)):
                for v, x in enumerate(jumps(out, ins, 2, sign, factor, speed[1], sound)):
                    dst[pl.ds(tile(v, a, b), 8), :] = get(dst, v, a, b) + x
            return carry

        lax.fori_loop(0, N, radial_faces, 0)

        def axial_faces(b, carry):
            lows = [get(src, v, 0, b) for v in range(V)]
            highs = [get(src, v, N - 1, b) for v in range(V)]
            below = [jnp.where(lane < SLAB, 0.0, roll(x, SLAB)) for x in highs]
            above = [jnp.where(lane >= LANES - SLAB, 0.0, roll(x, -SLAB)) for x in lows]
            factor = scale * LIFT
            for a, out, ins, sign in ((0, below, lows, 1.0), (N - 1, above, highs, -1.0)):
                for v, x in enumerate(jumps(out, ins, 3, sign, factor, speed[2], sound)):
                    dst[pl.ds(tile(v, a, b), 8), :] = get(dst, v, a, b) + x
            return carry

        lax.fori_loop(0, N, axial_faces, 0)

    def halo_faces(section, dst, scale):
        factor = scale * HALF * s1_6
        from_west = [east_in[section, v, pl.ds(0, N), :] for v in range(V)]
        from_east = [west_in[section, v, pl.ds(0, N), :] for v in range(V)]
        low = jumps(from_west, None, 1, 1.0, factor, speed[0], sound)
        high = jumps(from_east, None, 1, -1.0, factor, speed[0], sound)
        for v in range(V):
            for a in range(N):
                x = jnp.where(slot6 == 0, roll(low[v], -a), 0.0)
                dst[face(v, a, 0), :] = dst[face(v, a, 0), :] + x
                x = jnp.where(slot6 == EA - 1, roll(high[v], EA - 1 - a), 0.0)
                dst[face(v, a, N - 1), :] = dst[face(v, a, N - 1), :] + x

    def interface(section, digit, dst, scale):
        whole = lax.rem(frac_ref[section] // FRACS, EA)
        fraction = lax.rem(frac_ref[section], FRACS).astype(f32) / FRACS
        start = jnp.where(is_rotor, whole, EA - 1 - whole)
        scaled = by_sublane((POINTS + 1.0) / 2.0, N)
        rotor_up = jnp.where(scaled + fraction >= 1.0, 1.0, 0.0)
        stator_up = jnp.where(scaled > fraction, 1.0, 0.0)
        upper = jnp.where(is_rotor, rotor_up, stator_up)
        signed = jnp.where(is_rotor, scaled + fraction, scaled - fraction)
        base = jnp.where(is_rotor, 0.0, 1.0)
        local = (signed + base - upper) * 2.0 - 1.0
        weights = []
        for source in range(N):
            weight = jnp.ones_like(local)
            for another in range(N):
                if another != source:
                    weight = weight * (
                        (local - f32(POINTS[another]))
                        * f32(1.0 / (POINTS[source] - POINTS[another]))
                    )
            weights.append(weight)
        bits = [(start // s) % 2 == 1 for s in (1, 2, 4)]
        packed = []
        for t in range(8):
            held = [pair_in[section, h, pl.ds(N * t, N), :] for h in range(last_radix + 1)]
            first = choose(digit, held[1:])
            second = choose(digit, held[:-1])
            for bit, s in zip(bits, (1, 2, 4)):
                moved = jnp.where(slot6 < EA - s, roll(first, -s), roll(second, EA - s))
                first = jnp.where(bit, moved, first)
                second = jnp.where(bit, roll(second, -s), second)
            after = jnp.where(slot6 < EA - 1, roll(first, -1), roll(second, EA - 1))
            value = None
            for s in range(N):
                here = jnp.where(upper > 0.5, after[s : s + 1], first[s : s + 1])
                value = weights[s] * here if value is None else value + weights[s] * here
            packed.append(jnp.where(is_rotor, roll(value, LANES - SLAB), value))
        begin = jnp.where(is_rotor, LANES - SLAB, 0)
        valid = (lane6 >= begin) & (lane6 < begin + SLAB)
        sign = jnp.where(is_rotor, -1.0, 1.0)
        for b in range(N):
            outside = []
            for v in range(V):
                n = v * N + b
                outside.append(jnp.where(valid, roll(packed[n // 4], -SLAB * (n % 4)), 0.0))
            terms = jumps(outside, None, 3, sign, scale * LIFT, other_axial, other_sound)
            for v in range(V):
                rows = pl.ds(tile(v, own_a, b), N)
                dst[rows, :] = dst[rows, :] + terms[v]

    def run_section(section, src, dst, base, scale, ready=None):
        pack(src)
        if ready is not None:
            ready()
        first, halos = send_first(section)
        volume(src, dst, base, scale)
        last, digit = forward(section, first)
        inner_faces(src, dst, scale)
        for c in halos:
            c.wait()
        halo_faces(section, dst, scale)
        for c in last:
            c.wait()
        interface(section, digit, dst, scale)

    run_section(
        0,
        u_ref,
        w_ref,
        lambda v, a, b: get(u_ref, v, a, b),
        TIME_STEP,
        lambda: pl.semaphore_wait(barrier, len(targets)),
    )
    run_section(
        1,
        w_ref,
        u_ref,
        lambda v, a, b: 0.5 * (get(u_ref, v, a, b) + get(w_ref, v, a, b)),
        0.5 * TIME_STEP,
    )

    def store_state(a, carry):
        for v in range(V):
            for b in range(N):
                out_ref[v, a, b] = u_ref[pl.ds(tile(v, a, b), N), :]
        return carry

    lax.fori_loop(0, N, store_state, 0)


def solution(mesh):
    sectors = mesh.shape["sector"]
    stages = stages_of(sectors)
    n_sems = 2 + sum(radix for _, radix in stages) + len(stages)
    most = max(radix for _, radix in stages)

    def per_device(state, mean_flow, sector_offset, frac_index):
        table = jnp.asarray(DMAT, f32)
        smem = pl.BlockSpec(memory_space=pltpu.SMEM)
        vmem = pl.BlockSpec(memory_space=pltpu.VMEM)
        rows = V * N * N * 8
        return pl.pallas_call(
            functools.partial(kernel, sectors),
            out_shape=jax.ShapeDtypeStruct(state.shape, f32),
            in_specs=[smem, smem, smem, smem, vmem],
            out_specs=vmem,
            scratch_shapes=[
                pltpu.VMEM((rows, LANES), f32),
                pltpu.VMEM((rows, LANES), f32),
                pltpu.VMEM((V, 8, LANES), f32),
                pltpu.VMEM((V, 8, LANES), f32),
                pltpu.VMEM((2, V, 8, LANES), f32),
                pltpu.VMEM((2, V, 8, LANES), f32),
                pltpu.VMEM((TRACE_ROWS, LANES), f32),
                pltpu.VMEM((2, max(len(stages) - 1, 1), most, TRACE_ROWS, LANES), f32),
                pltpu.VMEM((2, stages[-1][1] + 1, TRACE_ROWS, LANES), f32),
                pltpu.SemaphoreType.DMA((2, n_sems)),
                pltpu.SemaphoreType.DMA((2, n_sems)),
            ],
            compiler_params=pltpu.CompilerParams(collective_id=0, has_side_effects=True),
        )(mean_flow, sector_offset, frac_index, table, state)

    spec = P(None, None, None, None, ("blk", "sector"))
    return jax.shard_map(
        per_device, mesh=mesh, in_specs=(spec, P(), P(), P()), out_specs=spec, check_vma=False
    )
```

profile of v0, /device:TPU:0, one launch (start us, length us, event | category | flops | bytes accessed | tf_op | source)
XLA Modules:
  0.0 30.3 jit_solution(5651008322079673241)
XLA Ops:
  0.0 28.3 %shard_map.55 = f32[5,6,6,6,128]{4,3,2,1,0:T(8,128)} custom-call(f32[2,4]{1,0:T(2,128)} %flow_ref.1, s32[2]{0:T(128)} %offset_ref.1, s32[2]{0:T(128)} %frac_ref.1, f32[6,6]{1,0:T(8,128)} %constant.2.clone.dtab_ref, f32[5,6,6,6,128]{4,3,2,1,0:T(8,128)} %state_ref.1), custom_call_target="tpu_custom_call" | custom-call | tf_op jit(solution)/shard_map/pallas_call | solution.py:454
  28.3 2.0 %copy.7 = f32[5,6,6,6,128]{4,3,2,1,0:T(8,128)} copy(f32[5,6,6,6,128]{4,3,2,1,0:T(8,128)} %shard_map.55) | data formatting | bytes 1105920
where the time goes:
time: 30.5 us; the launch traced here: 30.3 us
  Pallas kernels  28.3 us (93%)
  local copies, waits for them, and re-layouts  2.03 us (7%)
    pallas_call x1, Pallas kernels, per_device(): pl.pallas_call(functools.partial(kernel, sectors), out_shape=jax.ShapeDty...  28.3 us
    unnamed x1, local copies, waits for them, and re-layouts  2.03 us

commit v1 on v0

--- a/solution.py
+++ b/solution.py
@@ -51,14 +51,9 @@
 HALF = 0.5 * LIFT
 
 
-def stages_of(count):
-    digits = []
-    left = count
-    while left > 1:
-        radix = 4 if left % 4 == 0 else 2
-        left //= radix
-        digits.append((left, radix))
-    return digits
+def split_cycle(count):
+    group = math.gcd(count, 4)
+    return group, count // group
 
 
 def roll(x, by):
@@ -109,31 +104,32 @@
     east_in,
     trace_out,
     hop_in,
+    pair_out,
     pair_in,
     send_sem,
     recv_sem,
 ):
-    stages = stages_of(sectors)
+    group, groups = split_cycle(sectors)
     row = lax.axis_index("blk")
     me = lax.axis_index("sector")
+    member = lax.rem(me, group)
     is_rotor = row == 0
-    last_radix = stages[-1][1]
-
-    def at(flip, off):
-        return (1 - row if flip else row, lax.rem(me + off + sectors, sectors))
-
-    targets = [(0, -1)]
-    for s, (stride, radix) in enumerate(stages):
-        flip = 1 if s == 0 else 0
-        span = range(radix) if s == 0 else range(1, radix)
-        if s == len(stages) - 1:
-            span = range(1, radix + 1)
-        for h in span:
-            if (flip, h * stride) not in targets:
-                targets.append((flip, h * stride))
+
+    def around(off):
+        return (row, lax.rem(me + off + sectors, sectors))
+
+    def across(digit):
+        return (1 - row, lax.rem(me + digit * group, sectors))
+
+    def within(step):
+        return (row, me - member + lax.rem(member + step, group))
+
+    partners = [around(-1), around(1)]
+    partners += [across(h) for h in range(groups)]
+    partners += [within(g) for g in range(1, group)]
     barrier = pltpu.get_barrier_semaphore()
-    for flip, off in targets:
-        pl.semaphore_signal(barrier, inc=1, device_id=at(flip, -off), device_id_type=MESH)
+    for partner in partners:
+        pl.semaphore_signal(barrier, inc=1, device_id=partner, device_id_type=MESH)
 
     lane = lax.broadcasted_iota(jnp.int32, (8, LANES), 1)
     lane6 = lane[:N]
@@ -164,7 +160,7 @@
 
     lax.fori_loop(0, N, load_state, 0)
 
-    def pack(ref):
+    def pack_halo(ref):
         for v in range(V):
             left = jnp.zeros((N, LANES), f32)
             right = jnp.zeros((N, LANES), f32)
@@ -173,6 +169,8 @@
                 right = jnp.where(slot6 == a, roll(ref[face(v, a, N - 1), :], a - EA + 1), right)
             west_out[v, pl.ds(0, N), :] = left
             east_out[v, pl.ds(0, N), :] = right
+
+    def pack_trace(ref):
         quarter = lane6 // SLAB
         turned = jnp.where(is_rotor, (quarter + 1) % 4, quarter)
         for t in range(8):
@@ -194,45 +192,49 @@
             device_id_type=MESH,
         )
 
-    def send_first(section):
+    def send_across(section):
         copies = [
-            copy(section, 2 + h, trace_out, hop_in.at[section, 0, h], at(1, h * stages[0][0]))
-            for h in range(stages[0][1])
+            copy(section, 2 + h, trace_out, hop_in.at[section, h], across(h))
+            for h in reversed(range(groups))
         ]
-        halos = [
-            copy(section, 0, west_out, west_in.at[section], at(0, -1)),
-            copy(section, 1, east_out, east_in.at[section], at(0, 1)),
+        for c in copies:
+            c.start()
+        return copies
+
+    def send_halos(section):
+        copies = [
+            copy(section, 0, west_out, west_in.at[section], around(-1)),
+            copy(section, 1, east_out, east_in.at[section], around(1)),
         ]
-        for c in copies + halos:
+        for c in copies:
             c.start()
-        return copies, halos
-
-    def forward(section, copies):
+        return copies
+
+    def send_within(section):
         amount = jnp.where(
             is_rotor,
             lax.rem(2 * sectors - offset_ref[section] - 1, sectors),
             lax.rem(offset_ref[section], sectors),
         )
-        sem = 2 + stages[0][1]
-        for s in range(1, len(stages)):
-            for c in copies:
-                c.wait()
-            stride_before, radix_before = stages[s - 1]
-            digit = lax.rem(amount // stride_before, radix_before)
-            chosen = choose(digit, [hop_in[section, s - 1, h] for h in range(radix_before)])
-            stride, radix = stages[s]
-            if s == len(stages) - 1:
-                dst, span = pair_in.at[section], range(1, radix + 1)
-            else:
-                dst, span = hop_in.at[section, s], range(1, radix)
-            dst[0] = chosen
-            copies = []
-            for h in span:
-                copies.append(copy(section, sem, dst.at[0], dst.at[h], at(0, h * stride)))
-                sem += 1
-            for c in copies:
-                c.start()
-        return copies, lax.rem(amount, last_radix)
+        high, low = amount // group, lax.rem(amount, group)
+        arrived = [hop_in[section, h] for h in range(groups)]
+        facing = choose(lax.rem(high + (member + low) // group, groups), arrived)
+        prior = choose(lax.rem(high + (member + low + 1) // group, groups), arrived)
+        copies = []
+        for g in range(1, group):
+            pair_out[g - 1] = jnp.where(low == g, facing, prior)
+            copies.append(
+                copy(
+                    section,
+                    1 + groups + g,
+                    pair_out.at[g - 1],
+                    pair_in.at[section, g],
+                    within(g),
+                )
+            )
+            copies[-1].start()
+        pair_in[section, 0] = jnp.where(low == 0, facing, prior)
+        return copies, low
 
     def volume(src, dst, base, scale):
         k1 = -scale * s1 * speed[0]
@@ -374,9 +376,9 @@
         bits = [(start // s) % 2 == 1 for s in (1, 2, 4)]
         packed = []
         for t in range(8):
-            held = [pair_in[section, h, pl.ds(N * t, N), :] for h in range(last_radix + 1)]
-            first = choose(digit, held[1:])
-            second = choose(digit, held[:-1])
+            held = [pair_in[section, g, pl.ds(N * t, N), :] for g in range(group)]
+            first = choose(digit, held[1:] + held[:1])
+            second = choose(digit, held)
             for bit, s in zip(bits, (1, 2, 4)):
                 moved = jnp.where(slot6 < EA - s, roll(first, -s), roll(second, EA - s))
                 first = jnp.where(bit, moved, first)
@@ -401,13 +403,17 @@
                 dst[rows, :] = dst[rows, :] + terms[v]
 
     def run_section(section, src, dst, base, scale, ready=None):
-        pack(src)
+        pack_trace(src)
         if ready is not None:
             ready()
-        first, halos = send_first(section)
+        first = send_across(section)
+        pack_halo(src)
+        halos = send_halos(section)
         volume(src, dst, base, scale)
-        last, digit = forward(section, first)
         inner_faces(src, dst, scale)
+        for c in first:
+            c.wait()
+        last, digit = send_within(section)
         for c in halos:
             c.wait()
         halo_faces(section, dst, scale)
@@ -421,7 +427,7 @@
         w_ref,
         lambda v, a, b: get(u_ref, v, a, b),
         TIME_STEP,
-        lambda: pl.semaphore_wait(barrier, len(targets)),
+        lambda: pl.semaphore_wait(barrier, len(partners)),
     )
     run_section(
         1,
@@ -442,9 +448,8 @@
 
 def solution(mesh):
     sectors = mesh.shape["sector"]
-    stages = stages_of(sectors)
-    n_sems = 2 + sum(radix for _, radix in stages) + len(stages)
-    most = max(radix for _, radix in stages)
+    group, groups = split_cycle(sectors)
+    n_sems = 1 + groups + group
 
     def per_device(state, mean_flow, sector_offset, frac_index):
         table = jnp.asarray(DMAT, f32)
@@ -464,8 +469,9 @@
                 pltpu.VMEM((2, V, 8, LANES), f32),
                 pltpu.VMEM((2, V, 8, LANES), f32),
                 pltpu.VMEM((TRACE_ROWS, LANES), f32),
-                pltpu.VMEM((2, max(len(stages) - 1, 1), most, TRACE_ROWS, LANES), f32),
-                pltpu.VMEM((2, stages[-1][1] + 1, TRACE_ROWS, LANES), f32),
+                pltpu.VMEM((2, groups, TRACE_ROWS, LANES), f32),
+                pltpu.VMEM((max(group - 1, 1), TRACE_ROWS, LANES), f32),
+                pltpu.VMEM((2, group, TRACE_ROWS, LANES), f32),
                 pltpu.SemaphoreType.DMA((2, n_sems)),
                 pltpu.SemaphoreType.DMA((2, n_sems)),
             ],

time: 30.5 us -> 26.8 us (0.88)
  Pallas kernels: 28.3 us -> 24.6 us
    pallas_call x1, Pallas kernels: 28.3 us -> 24.6 us  [per_device(): pl.pallas_call(functools.partial(kernel, sectors), out_shape=jax.ShapeDty...]
where the time goes in v1:
time: 26.8 us; the launch traced here: 26.6 us
  Pallas kernels  24.6 us (92%)
  local copies, waits for them, and re-layouts  2.03 us (8%)
    pallas_call x1, Pallas kernels, per_device(): pl.pallas_call(functools.partial(kernel, sectors), out_shape=jax.ShapeDty...  24.6 us
    unnamed x1, local copies, waits for them, and re-layouts  2.03 us

profile of v1, /device:TPU:0, one launch (start us, length us, event | category | flops | bytes accessed | tf_op | source)
XLA Modules:
  0.0 26.6 jit_solution(16939081313761303393)
XLA Ops:
  0.0 24.6 %shard_map.55 = f32[5,6,6,6,128]{4,3,2,1,0:T(8,128)} custom-call(f32[2,4]{1,0:T(2,128)} %flow_ref.1, s32[2]{0:T(128)} %offset_ref.1, s32[2]{0:T(128)} %frac_ref.1, f32[6,6]{1,0:T(8,128)} %constant.2.clone.dtab_ref, f32[5,6,6,6,128]{4,3,2,1,0:T(8,128)} %state_ref.1), custom_call_target="tpu_custom_call" | custom-call | tf_op jit(solution)/shard_map/pallas_call | solution.py:459
  24.6 2.0 %copy.7 = f32[5,6,6,6,128]{4,3,2,1,0:T(8,128)} copy(f32[5,6,6,6,128]{4,3,2,1,0:T(8,128)} %shard_map.55) | data formatting | bytes 1105920

commit v2 on v1

--- a/solution.py
+++ b/solution.py
@@ -90,12 +90,16 @@
 
 def kernel(
     sectors,
+    flow_hbm,
+    offset_hbm,
+    frac_hbm,
+    state_hbm,
+    out_ref,
     flow_ref,
     offset_ref,
     frac_ref,
-    dtab_ref,
     state_ref,
-    out_ref,
+    face_ref,
     u_ref,
     w_ref,
     west_out,
@@ -106,6 +110,7 @@
     hop_in,
     pair_out,
     pair_in,
+    load_sem,
     send_sem,
     recv_sem,
 ):
@@ -131,12 +136,31 @@
     for partner in partners:
         pl.semaphore_signal(barrier, inc=1, device_id=partner, device_id_type=MESH)
 
+    own_a = jnp.where(is_rotor, N - 1, 0)
+    loads = [
+        pltpu.make_async_copy(src, dst, load_sem.at[k])
+        for k, (src, dst) in enumerate(
+            (
+                (state_hbm.at[:, own_a], face_ref),
+                (flow_hbm, flow_ref),
+                (offset_hbm, offset_ref),
+                (frac_hbm, frac_ref),
+                (state_hbm, state_ref),
+            )
+        )
+    ]
+    for c in loads:
+        c.start()
+
     lane = lax.broadcasted_iota(jnp.int32, (8, LANES), 1)
     lane6 = lane[:N]
     slot6 = lane6 % EA
     radial = (lane // EA) % ER
     s1 = 2.0 / (1.0 + (radial.astype(f32) + 0.5) / ER)
     s1_6 = s1[:N]
+
+    for c in loads[1:4]:
+        c.wait()
 
     def pick(k):
         return jnp.where(is_rotor, flow_ref[0, k], flow_ref[1, k])
@@ -150,15 +174,11 @@
         jnp.maximum(jnp.abs(flow_ref[0, k]), jnp.abs(flow_ref[1, k])) + top_sound for k in range(3)
     ]
     dcols = [by_sublane(DMAT[:, j], 8) for j in range(N)]
-    own_a = jnp.where(is_rotor, N - 1, 0)
-
     def load_state(a, carry):
         for v in range(V):
             for b in range(N):
                 u_ref[pl.ds(tile(v, a, b), N), :] = state_ref[v, a, b]
         return carry
-
-    lax.fori_loop(0, N, load_state, 0)
 
     def pack_halo(ref):
         for v in range(V):
@@ -170,7 +190,7 @@
             west_out[v, pl.ds(0, N), :] = left
             east_out[v, pl.ds(0, N), :] = right
 
-    def pack_trace(ref):
+    def pack_trace(read):
         quarter = lane6 // SLAB
         turned = jnp.where(is_rotor, (quarter + 1) % 4, quarter)
         for t in range(8):
@@ -178,7 +198,7 @@
             for q in range(4):
                 n = 4 * t + q
                 if n < V * N:
-                    here = ref[pl.ds(tile(n // N, own_a, n % N), N), :]
+                    here = read(n // N, n % N)
                     merged = jnp.where(turned == q, roll(here, SLAB * q), merged)
             trace_out[pl.ds(N * t, N), :] = jnp.where(is_rotor, roll(merged, SLAB), merged)
 
@@ -195,7 +215,7 @@
     def send_across(section):
         copies = [
             copy(section, 2 + h, trace_out, hop_in.at[section, h], across(h))
-            for h in reversed(range(groups))
+            for h in sorted(range(groups), key=lambda h: -min(h, groups - h))
         ]
         for c in copies:
             c.start()
@@ -244,7 +264,7 @@
         c2 = jnp.full((8, LANES), -2.0 * scale * sound, f32)
 
         def at_b(b, carry):
-            row_b = [dtab_ref[b, j] for j in range(N)]
+            row_b = [choose(b, [f32(DMAT[k, j]) for k in range(N)]) for j in range(N)]
             for a in range(N):
                 kept = {}
                 zero_sum = None
@@ -402,11 +422,7 @@
                 rows = pl.ds(tile(v, own_a, b), N)
                 dst[rows, :] = dst[rows, :] + terms[v]
 
-    def run_section(section, src, dst, base, scale, ready=None):
-        pack_trace(src)
-        if ready is not None:
-            ready()
-        first = send_across(section)
+    def run_section(section, first, src, dst, base, scale):
         pack_halo(src)
         halos = send_halos(section)
         volume(src, dst, base, scale)
@@ -421,16 +437,17 @@
             c.wait()
         interface(section, digit, dst, scale)
 
-    run_section(
-        0,
-        u_ref,
-        w_ref,
-        lambda v, a, b: get(u_ref, v, a, b),
-        TIME_STEP,
-        lambda: pl.semaphore_wait(barrier, len(partners)),
-    )
+    loads[0].wait()
+    pack_trace(lambda v, b: face_ref[v, b])
+    pl.semaphore_wait(barrier, len(partners))
+    first = send_across(0)
+    loads[4].wait()
+    lax.fori_loop(0, N, load_state, 0)
+    run_section(0, first, u_ref, w_ref, lambda v, a, b: get(u_ref, v, a, b), TIME_STEP)
+    pack_trace(lambda v, b: w_ref[pl.ds(tile(v, own_a, b), N), :])
     run_section(
         1,
+        send_across(1),
         w_ref,
         u_ref,
         lambda v, a, b: 0.5 * (get(u_ref, v, a, b) + get(w_ref, v, a, b)),
@@ -452,16 +469,20 @@
     n_sems = 1 + groups + group
 
     def per_device(state, mean_flow, sector_offset, frac_index):
-        table = jnp.asarray(DMAT, f32)
-        smem = pl.BlockSpec(memory_space=pltpu.SMEM)
+        hbm = pl.BlockSpec(memory_space=pltpu.HBM)
         vmem = pl.BlockSpec(memory_space=pltpu.VMEM)
         rows = V * N * N * 8
         return pl.pallas_call(
             functools.partial(kernel, sectors),
-            out_shape=jax.ShapeDtypeStruct(state.shape, f32),
-            in_specs=[smem, smem, smem, smem, vmem],
+            out_shape=pltpu.VMEM(state.shape, f32),
+            in_specs=[hbm, hbm, hbm, hbm],
             out_specs=vmem,
             scratch_shapes=[
+                pltpu.SMEM(mean_flow.shape, f32),
+                pltpu.SMEM(sector_offset.shape, jnp.int32),
+                pltpu.SMEM(frac_index.shape, jnp.int32),
+                pltpu.VMEM(state.shape, f32),
+                pltpu.VMEM((V, N, N, LANES), f32),
                 pltpu.VMEM((rows, LANES), f32),
                 pltpu.VMEM((rows, LANES), f32),
                 pltpu.VMEM((V, 8, LANES), f32),
@@ -472,11 +493,12 @@
                 pltpu.VMEM((2, groups, TRACE_ROWS, LANES), f32),
                 pltpu.VMEM((max(group - 1, 1), TRACE_ROWS, LANES), f32),
                 pltpu.VMEM((2, group, TRACE_ROWS, LANES), f32),
+                pltpu.SemaphoreType.DMA((5,)),
                 pltpu.SemaphoreType.DMA((2, n_sems)),
                 pltpu.SemaphoreType.DMA((2, n_sems)),
             ],
             compiler_params=pltpu.CompilerParams(collective_id=0, has_side_effects=True),
-        )(mean_flow, sector_offset, frac_index, table, state)
+        )(mean_flow, sector_offset, frac_index, state)
 
     spec = P(None, None, None, None, ("blk", "sector"))
     return jax.shard_map(

time: 26.8 us -> 23.9 us (0.89)
  Pallas kernels: 24.6 us -> 22.8 us
  local copies, waits for them, and re-layouts: 2.03 us -> 0.87 us
    pallas_call x1, Pallas kernels: 24.6 us -> 22.8 us  [per_device(): pl.pallas_call(functools.partial(kernel, sectors), out_shape=pltpu.VMEM(s...]
    unnamed x1, local copies, waits for them, and re-layouts: 2.03 us -> 0.87 us
where the time goes in v2:
time: 23.9 us; the launch traced here: 23.7 us
  Pallas kernels  22.8 us (95%)
  local copies, waits for them, and re-layouts  0.87 us (4%)
    pallas_call x1, Pallas kernels, per_device(): pl.pallas_call(functools.partial(kernel, sectors), out_shape=pltpu.VMEM(s...  22.8 us
    unnamed x1, local copies, waits for them, and re-layouts  0.87 us

profile of v2, /device:TPU:0, one launch (start us, length us, event | category | flops | bytes accessed | tf_op | source)
XLA Modules:
  0.0 23.7 jit_solution(15807493054167371319)
XLA Ops:
  0.0 22.8 %shard_map.46 = f32[5,6,6,6,128]{4,3,2,1,0:T(8,128)S(1)} custom-call(f32[2,4]{1,0:T(2,128)} %flow_hbm.1, s32[2]{0:T(128)} %offset_hbm.1, s32[2]{0:T(128)} %frac_hbm.1, f32[5,6,6,6,128]{4,3,2,1,0:T(8,128)} %state_hbm.1), custom_call_target="tpu_custom_call" | custom-call | tf_op jit(solution)/shard_map/pallas_call | solution.py:475
  22.9 0.9 %copy.6 = f32[5,6,6,6,128]{4,3,2,1,0:T(8,128)} copy(f32[5,6,6,6,128]{4,3,2,1,0:T(8,128)S(1)} %shard_map.46) | data formatting | bytes 1105920

commit v3 on v2

--- a/solution.py
+++ b/solution.py
@@ -59,6 +59,10 @@
 def roll(x, by):
     by = by % LANES
     return x if by == 0 else pltpu.roll(x, by, 1)
+
+
+def turn(x, by):
+    return pltpu.roll(x, lax.rem(by + 2 * LANES, LANES), 1)
 
 
 def tile(v, a, b):
@@ -241,7 +245,7 @@
         facing = choose(lax.rem(high + (member + low) // group, groups), arrived)
         prior = choose(lax.rem(high + (member + low + 1) // group, groups), arrived)
         copies = []
-        for g in range(1, group):
+        for g in sorted(range(1, group), key=lambda g: -min(g, group - g)):
             pair_out[g - 1] = jnp.where(low == g, facing, prior)
             copies.append(
                 copy(
@@ -372,7 +376,7 @@
                 x = jnp.where(slot6 == EA - 1, roll(high[v], EA - 1 - a), 0.0)
                 dst[face(v, a, N - 1), :] = dst[face(v, a, N - 1), :] + x
 
-    def interface(section, digit, dst, scale):
+    def mortar(section):
         whole = lax.rem(frac_ref[section] // FRACS, EA)
         fraction = lax.rem(frac_ref[section], FRACS).astype(f32) / FRACS
         start = jnp.where(is_rotor, whole, EA - 1 - whole)
@@ -393,22 +397,24 @@
                         * f32(1.0 / (POINTS[source] - POINTS[another]))
                     )
             weights.append(weight)
-        bits = [(start // s) % 2 == 1 for s in (1, 2, 4)]
+        return upper, weights, start
+
+    def interface(section, digit, tables, dst, scale):
+        upper, weights, start = tables
         packed = []
         for t in range(8):
             held = [pair_in[section, g, pl.ds(N * t, N), :] for g in range(group)]
             first = choose(digit, held[1:] + held[:1])
             second = choose(digit, held)
-            for bit, s in zip(bits, (1, 2, 4)):
-                moved = jnp.where(slot6 < EA - s, roll(first, -s), roll(second, EA - s))
-                first = jnp.where(bit, moved, first)
-                second = jnp.where(bit, roll(second, -s), second)
-            after = jnp.where(slot6 < EA - 1, roll(first, -1), roll(second, EA - 1))
+            lower = jnp.where(slot6 < EA - start, turn(first, -start), turn(second, EA - start))
+            after = jnp.where(
+                slot6 < EA - 1 - start, turn(first, -start - 1), turn(second, EA - 1 - start)
+            )
             value = None
             for s in range(N):
-                here = jnp.where(upper > 0.5, after[s : s + 1], first[s : s + 1])
+                here = jnp.where(upper > 0.5, after[s : s + 1], lower[s : s + 1])
                 value = weights[s] * here if value is None else value + weights[s] * here
-            packed.append(jnp.where(is_rotor, roll(value, LANES - SLAB), value))
+            packed.append(value)
         begin = jnp.where(is_rotor, LANES - SLAB, 0)
         valid = (lane6 >= begin) & (lane6 < begin + SLAB)
         sign = jnp.where(is_rotor, -1.0, 1.0)
@@ -416,26 +422,34 @@
             outside = []
             for v in range(V):
                 n = v * N + b
-                outside.append(jnp.where(valid, roll(packed[n // 4], -SLAB * (n % 4)), 0.0))
+                outside.append(jnp.where(valid, turn(packed[n // 4], begin - SLAB * (n % 4)), 0.0))
             terms = jumps(outside, None, 3, sign, scale * LIFT, other_axial, other_sound)
             for v in range(V):
                 rows = pl.ds(tile(v, own_a, b), N)
                 dst[rows, :] = dst[rows, :] + terms[v]
 
-    def run_section(section, first, src, dst, base, scale):
+    def run_section(section, first, src, dst, base, scale, early):
         pack_halo(src)
         halos = send_halos(section)
         volume(src, dst, base, scale)
         inner_faces(src, dst, scale)
+        tables = mortar(section)
         for c in first:
             c.wait()
         last, digit = send_within(section)
         for c in halos:
             c.wait()
         halo_faces(section, dst, scale)
+        early()
         for c in last:
             c.wait()
-        interface(section, digit, dst, scale)
+        interface(section, digit, tables, dst, scale)
+
+    def store_layer(a, carry):
+        for v in range(V):
+            for b in range(N):
+                out_ref[v, a, b] = u_ref[pl.ds(tile(v, a, b), N), :]
+        return carry
 
     loads[0].wait()
     pack_trace(lambda v, b: face_ref[v, b])
@@ -443,7 +457,7 @@
     first = send_across(0)
     loads[4].wait()
     lax.fori_loop(0, N, load_state, 0)
-    run_section(0, first, u_ref, w_ref, lambda v, a, b: get(u_ref, v, a, b), TIME_STEP)
+    run_section(0, first, u_ref, w_ref, lambda v, a, b: get(u_ref, v, a, b), TIME_STEP, lambda: None)
     pack_trace(lambda v, b: w_ref[pl.ds(tile(v, own_a, b), N), :])
     run_section(
         1,
@@ -452,15 +466,9 @@
         u_ref,
         lambda v, a, b: 0.5 * (get(u_ref, v, a, b) + get(w_ref, v, a, b)),
         0.5 * TIME_STEP,
+        lambda: lax.fori_loop(0, N, store_layer, 0),
     )
-
-    def store_state(a, carry):
-        for v in range(V):
-            for b in range(N):
-                out_ref[v, a, b] = u_ref[pl.ds(tile(v, a, b), N), :]
-        return carry
-
-    lax.fori_loop(0, N, store_state, 0)
+    store_layer(own_a, 0)
 
 
 def solution(mesh):

time: 23.9 us -> 23.2 us (0.971)
  Pallas kernels: 22.8 us -> 22.2 us
    pallas_call x1, Pallas kernels: 22.8 us -> 22.2 us  [per_device(): pl.pallas_call(functools.partial(kernel, sectors), out_shape=pltpu.VMEM(s...]
where the time goes in v3:
time: 23.2 us; the launch traced here: 23.1 us
  Pallas kernels  22.2 us (96%)
  local copies, waits for them, and re-layouts  0.87 us (4%)
    pallas_call x1, Pallas kernels, per_device(): pl.pallas_call(functools.partial(kernel, sectors), out_shape=pltpu.VMEM(s...  22.2 us
    unnamed x1, local copies, waits for them, and re-layouts  0.87 us

profile of v3, /device:TPU:0, one launch (start us, length us, event | category | flops | bytes accessed | tf_op | source)
XLA Modules:
  0.0 23.1 jit_solution(13612980672502212540)
XLA Ops:
  0.0 22.2 %shard_map.46 = f32[5,6,6,6,128]{4,3,2,1,0:T(8,128)S(1)} custom-call(f32[2,4]{1,0:T(2,128)} %flow_hbm.1, s32[2]{0:T(128)} %offset_hbm.1, s32[2]{0:T(128)} %frac_hbm.1, f32[5,6,6,6,128]{4,3,2,1,0:T(8,128)} %state_hbm.1), custom_call_target="tpu_custom_call" | custom-call | tf_op jit(solution)/shard_map/pallas_call | solution.py:483
  22.2 0.9 %copy.6 = f32[5,6,6,6,128]{4,3,2,1,0:T(8,128)} copy(f32[5,6,6,6,128]{4,3,2,1,0:T(8,128)S(1)} %shard_map.46) | data formatting | bytes 1105920
